TPU v7x, 32 devices: a whole 2x2x4 slice. The times are simulated.
32 devices in a mesh: dp: 4 (over y, x), mp: 8 (over z, core).
Axes of the slice: x: 2, y: 2, z: 4, core: 2. Of those that a mesh axis runs over, the one named last changes fastest.
Arguments:
- residual_in: bfloat16 [512, 3584], P('dp', 'mp'), may hold values from -6 to 6
- pre_gain: float32 [3584], replicated, may hold values from 0.5 to 1.5
- post_gain: float32 [3584], replicated, may hold values from 0.5 to 1.5
- w_gate: bfloat16 [3584, 14336], P(None, 'mp'), may hold values from -0.09375 to 0.09375
- w_up: bfloat16 [3584, 14336], P(None, 'mp'), may hold values from -0.09375 to 0.09375
- w_down: bfloat16 [14336, 3584], P('mp'), may hold values from -0.046875 to 0.046875
- w_enc: bfloat16 [3584, 16384], P(None, ('dp', 'mp')), may hold values from -0.09375 to 0.09375
- b_enc: float32 [16384], P(('dp', 'mp')), may hold values from -2.5 to 2.5
- threshold: float32 [16384], P(('dp', 'mp')), may hold values from 0.1 to 1
- w_dec: bfloat16 [16384, 3584], P(('dp', 'mp')), may hold values from -0.046875 to 0.046875
- b_dec: float32 [3584], replicated, may hold values from -1.5 to 1.5
Outputs:
- loss_value: float32 [], replicated
- d_w_enc: bfloat16 [3584, 16384], P(None, ('dp', 'mp'))
- d_w_dec: bfloat16 [16384, 3584], P(('dp', 'mp'))
- d_b_enc: float32 [16384], P(('dp', 'mp'))
- d_threshold: float32 [16384], P(('dp', 'mp'))
- d_b_dec: float32 [3584], replicated
All inputs are finite; a program needn't handle non-finite values.
Results may differ from a plain program's by a relative error of at most 0.014.
The roundings to bfloat16 on the way count: a program that leaves them out, or rounds other values in their place, can miss the bound.
Values may be sent and summed in bfloat16 or wider, within the bound.
No kernel may reach another device: no remote copies, remote signals or barrier semaphores. Data moves between devices by JAX's collectives and lax.ppermute only.
A program may use at most 128 MiB of HBM per device.

v0:
```python
import jax
import jax.numpy as jnp
from jax import lax
from jax.sharding import PartitionSpec as P

norm_eps = 1e-06
gate_band = 0.1
sparsity_coef = 0.05


def contract_first(left, right):
    return lax.dot_general(
        left, right, (((0,), (0,)), ((), ())), preferred_element_type=jnp.float32
    )


def local(
    residual_in, pre_gain, post_gain, w_gate, w_up, w_down, w_enc, b_enc, threshold, w_dec, b_dec
):
    full_rows = lax.all_gather(residual_in, "mp", axis=1, tiled=True)
    resid_wide = full_rows.astype(jnp.float32)
    normed = (
        resid_wide
        * lax.rsqrt(jnp.mean(resid_wide * resid_wide, axis=1, keepdims=True) + norm_eps)
        * pre_gain[None, :]
    ).astype(jnp.bfloat16)
    gate_out = jnp.dot(normed, w_gate, preferred_element_type=jnp.float32)
    up_out = jnp.dot(normed, w_up, preferred_element_type=jnp.float32)
    hidden = (jax.nn.gelu(gate_out, approximate=True) * up_out).astype(jnp.bfloat16)
    out_share = lax.psum_scatter(
        lax.dot_general(
            w_down, hidden, (((0,), (1,)), ((), ())), preferred_element_type=jnp.float32
        ),
        "mp",
        scatter_dimension=0,
        tiled=True,
    )
    whole_out = lax.all_gather(out_share, "mp", axis=0, tiled=True)
    row_scale = lax.rsqrt(jnp.mean(whole_out * whole_out, axis=0) + norm_eps)
    mixed = resid_wide.T + whole_out * row_scale[None, :] * post_gain[:, None]
    column_rows = mixed.astype(jnp.bfloat16)
    h_cols = lax.all_gather(column_rows, "dp", axis=1, tiled=True)
    pre_act = contract_first(h_cols, w_enc) + b_enc[None, :]
    soft = jax.nn.sigmoid((pre_act - threshold[None, :]) / gate_band)
    feat_bf = (pre_act * soft).astype(jnp.bfloat16)
    gate_part = jnp.sum(soft)
    recon_part = lax.dot_general(
        w_dec, feat_bf, (((0,), (1,)), ((), ())), preferred_element_type=jnp.float32
    )
    recon_all, gate_total = lax.psum((recon_part, gate_part), ("dp", "mp"))
    error_t = recon_all + b_dec[:, None] - h_cols.astype(jnp.float32)
    grad_bdec = jnp.sum(error_t, axis=1)
    square_total = jnp.sum(error_t * error_t)
    err_bf = error_t.astype(jnp.bfloat16)
    loss_value = (0.5 * square_total + sparsity_coef * gate_total) / (
        h_cols.shape[0] * h_cols.shape[1]
    )
    grad_wdec = lax.dot_general(
        feat_bf, err_bf, (((0,), (1,)), ((), ())), preferred_element_type=jnp.float32
    ).astype(jnp.bfloat16)
    grad_feat = lax.dot_general(
        err_bf, w_dec, (((0,), (1,)), ((), ())), preferred_element_type=jnp.float32
    )
    slope = soft * (1.0 - soft) / gate_band
    side_term = (grad_feat * pre_act + sparsity_coef) * slope
    grad_pre = grad_feat * soft + side_term
    grad_thresh = -jnp.sum(side_term, axis=0)
    grad_benc = jnp.sum(grad_pre, axis=0)
    grad_wenc = jnp.dot(
        h_cols, grad_pre.astype(jnp.bfloat16), preferred_element_type=jnp.float32
    ).astype(jnp.bfloat16)
    return (loss_value, grad_wenc, grad_wdec, grad_benc, grad_thresh, grad_bdec)


def solution(mesh):
    placed = (
        P("dp", "mp"),
        P(),
        P(),
        P(None, "mp"),
        P(None, "mp"),
        P("mp", None),
        P(None, ("dp", "mp")),
        P(("dp", "mp")),
        P(("dp", "mp")),
        P(("dp", "mp"), None),
        P(),
    )
    return jax.shard_map(
        local,
        mesh=mesh,
        in_specs=placed,
        out_specs=(
            P(),
            P(None, ("dp", "mp")),
            P(("dp", "mp"), None),
            P(("dp", "mp")),
            P(("dp", "mp")),
            P(),
        ),
        check_vma=False,
    )
```

profile of v0, /device:TPU:0, one launch (start us, length us, event | category | flops | bytes accessed | tf_op | source)
XLA Modules:
  0.0 411.2 jit_solution(16962882458070409448)
XLA Ops:
  7.2 0.0 reduce-scatter.4.cloned.1.call-start
  7.2 17.8 %all_gather.9 = bf16[128,3584]{0,1:T(8,128)(2,1)S(1)} all-gather(bf16[128,448]{0,1:T(8,128)(2,1)} %param.11), channel_id=1, replica_groups=mesh['dp'=4,'mp'=8] {'mp'}, dimensions={1}, use_global_device_ids=true | all-gather | bytes 1032192 | tf_op jit(solution)/shard_map/all_gather | solution.py:20
  25.1 0.5 copy.18
  25.6 0.3 fusion.5
  25.9 7.5 %fusion.25 = f32[128,1792]{1,0:T(8,128)} fusion(bf16[3584,1792]{1,0:T(8,128)(2,1)} %param.14, bf16[128,3584]{1,0:T(8,128)(2,1)S(1)} %copy.18, f32[3584]{0:T(1024)S(1)} %copy-done, f32[128]{0:T(128)S(1)} %add_rsqrt_fusion.1), kind=kOutput, calls=%fused_computation.40 | convolution fusion | flops 1646002176 | bytes 14694912 | tf_op jit(solution)/shard_map/dot_general | solution.py:27
  33.3 12.8 %convolution_bitcast_fusion.1 = f32[3584,128]{0,1:T(8,128)S(1)} fusion(bf16[1792,3584]{1,0:T(8,128)(2,1)} %param.16, bf16[3584,1792]{1,0:T(8,128)(2,1)} %param.15, f32[128,1792]{1,0:T(8,128)} %fusion.25, bf16[128,3584]{1,0:T(8,128)(2,1)S(1)} %copy.18, f32[3584]{0:T(1024)S(1)} %copy-done, f32[128]{0:T(128)S(1)} %add_rsqrt_fusion.1), kind=kOutput, calls=%fused_computation.5 | convolution fusion | flops 3292463104 | bytes 29374976 | tf_op jit(solution)/shard_map/dot_general | solution.py:31
  46.1 1.7 copy.21
  47.8 0.0 all-gather.3.cloned.1.call-start
  47.9 36.9 %reduce-scatter.4.cloned.1.call-done = f32[448,128]{1,0:T(8,128)} async-done(((f32[3584,128]{1,0:T(8,128)}), f32[448,128]{1,0:T(8,128)}) %reduce-scatter.4.cloned.1.call-update) | async-done | bytes 229392 | tf_op jit(solution)/shard_map/reduce_scatter | solution.py:30
  84.8 26.5 %all-gather.3.cloned.1.call-done = f32[3584,128]{1,0:T(8,128)} async-done(((f32[448,128]{1,0:T(8,128)}), f32[3584,128]{1,0:T(8,128)}) %all-gather.3.cloned.1.call-update) | async-done | bytes 1835024 | tf_op jit(solution)/shard_map/all_gather | solution.py:38
  111.4 2.0 multiply_reduce_fusion.1
  113.4 1.8 copy.20
  115.2 1.3 fusion.4
  116.5 0.2 all-reduce.2.cloned.1.call-start
  116.7 47.5 %all-gather.5.cloned.1.call-done = bf16[3584,512]{0,1:T(8,128)(2,1)} async-done(((bf16[3584,128]{0,1:T(8,128)(2,1)}), bf16[3584,512]{0,1:T(8,128)(2,1)}) %all-gather.5.cloned.1.call-update) | async-done | bytes 3670032 | tf_op jit(solution)/shard_map/all_gather | solution.py:42
  164.3 5.3 %convolution_add_fusion = f32[512,512]{1,0:T(8,128)S(1)} fusion(bf16[3584,512]{0,1:T(8,128)(2,1)} %all-gather.5.cloned.1.call-done, bf16[3584,512]{1,0:T(8,128)(2,1)} %param.17, f32[512]{0:T(512)S(1)} %copy-done.5), kind=kOutput, calls=%fused_computation.21 | convolution fusion | flops 1879310336 | bytes 8390656 | tf_op jit(solution)/shard_map/dot_general | solution.py:12
  169.6 5.1 %convolution_bitcast_fusion = f32[3584,512]{0,1:T(8,128)} fusion(bf16[512,3584]{1,0:T(8,128)(2,1)S(1)} %copy-done.3, f32[512,512]{1,0:T(8,128)S(1)} %convolution_add_fusion, f32[512]{0:T(512)S(1)} %copy-done.6), kind=kOutput, calls=%fused_computation.2 | convolution fusion | flops 1880883200 | bytes 12060672 | tf_op jit(solution)/shard_map/dot_general | solution.py:47
  174.8 167.4 %all-reduce.2.cloned.1.call-done = f32[3584,512]{0,1:T(8,128)} async-done(((f32[3584,512]{0,1:T(8,128)}), f32[3584,512]{0,1:T(8,128)}) %all-reduce.2.cloned.1.call-update) | async-done | bytes 7340048 | tf_op jit(solution)/shard_map/psum | solution.py:50
  342.2 5.9 %fusion.1 = (f32[3584]{0:T(1024)}, f32[]{:T(128)}, bf16[3584,512]{0,1:T(8,128)(2,1)S(1)}) fusion(bf16[3584,512]{0,1:T(8,128)(2,1)} %all-gather.5.cloned.1.call-done, f32[3584,512]{0,1:T(8,128)} %all-reduce.2.cloned.1.call-done, f32[3584]{0:T(1024)S(1)} %copy-done.2), kind=kLoop, calls=%fused_computation.11 | loop fusion | flops 12841471 | bytes 14708740 | tf_op jit(solution)/shard_map/reduce_sum | solution.py:52
  348.2 3.1 fusion.32
  351.2 4.0 convolution_convert_fusion
  355.2 40.4 %psum.15 = f32[]{:T(128)} all-reduce(f32[]{:T(128)} %get-tuple-element.13), channel_id=1, replica_groups=mesh['dp'=4,'mp'=8] {'dp','mp'}, use_global_device_ids=true, to_apply=%region_6.0 | all-reduce | flops 1 | bytes 8 | tf_op jit(solution)/shard_map/psum | solution.py:50
  395.7 0.6 neg.7
  397.6 6.0 %convolution_convert_fusion.1 = bf16[3584,512]{1,0:T(8,128)(2,1)} fusion(bf16[3584,512]{0,1:T(8,128)(2,1)} %all-gather.5.cloned.1.call-done, bf16[512,512]{1,0:T(8,128)(2,1)S(1)} %get-tuple-element.11), kind=kOutput, calls=%fused_computation.4 | convolution fusion | flops 1880883200 | bytes 7864320 | tf_op jit(solution)/shard_map/dot_general | solution.py:69
  (21 shorter events, 0.1 us)
Async XLA Ops:
  7.2 18.7 %copy-start = (f32[3584]{0:T(1024)S(1)}, f32[3584]{0:T(1024)}, u32[]{:S(2)}) copy-start(f32[3584]{0:T(1024)} %param.12) | copy-start | bytes 43012
  7.2 77.6 %reduce-scatter.4.cloned.1.call-start = ((), (), s32[]{:S(2)}) async-start(), calls=%async_computation.4 | async-start | bytes 2064384 | tf_op jit(solution)/shard_map/reduce_scatter | solution.py:30
  47.8 67.4 %copy-start.1 = (f32[3584]{0:T(1024)S(1)}, f32[3584]{0:T(1024)}, u32[]{:S(2)}) copy-start(f32[3584]{0:T(1024)} %param.13) | copy-start | bytes 43012
  47.8 63.5 %all-gather.3.cloned.1.call-start = ((), (), s32[]{:S(2)}) async-start(), calls=%async_computation.1 | async-start | bytes 2064384 | tf_op jit(solution)/shard_map/all_gather | solution.py:38
  84.8 79.5 %all-gather.5.cloned.1.call-start = ((), (), s32[]{:S(2)}) async-start(), calls=%async_computation.2 | async-start | bytes 4587520 | tf_op jit(solution)/shard_map/all_gather | solution.py:42
  113.4 50.9 %copy-start.5 = (f32[512]{0:T(512)S(1)}, f32[512]{0:T(512)}, u32[]{:S(2)}) copy-start(f32[512]{0:T(512)} %param.18) | copy-start | bytes 6148
  116.5 53.1 %copy-start.6 = (f32[512]{0:T(512)S(1)}, f32[512]{0:T(512)}, u32[]{:S(2)}) copy-start(f32[512]{0:T(512)} %param.19) | copy-start | bytes 6148
  116.5 225.7 %all-reduce.2.cloned.1.call-start = ((), (), s32[]{:S(2)}) async-start(), calls=%async_computation.3 | async-start | bytes 14680064 | tf_op jit(solution)/shard_map/psum | solution.py:50
  164.3 5.4 %copy-start.3 = (bf16[512,3584]{1,0:T(8,128)(2,1)S(1)}, bf16[512,3584]{1,0:T(8,128)(2,1)}, u32[]{:S(2)}) copy-start(bf16[512,3584]{1,0:T(8,128)(2,1)} %param.20) | copy-start | bytes 11010052
  174.8 167.4 %copy-start.2 = (f32[3584]{0:T(1024)S(1)}, f32[3584]{0:T(1024)}, u32[]{:S(2)}) copy-start(f32[3584]{0:T(1024)} %param.21) | copy-start | bytes 43012
  342.2 5.9 %copy-start.4 = (bf16[512,3584]{1,0:T(8,128)(2,1)S(1)}, bf16[512,3584]{1,0:T(8,128)(2,1)}, u32[]{:S(2)}) copy-start(bf16[512,3584]{1,0:T(8,128)(2,1)} %param.20) | copy-start | bytes 11010052
Sparse Core Ops, SparseCore 0:
  48.0 36.7 reduce-scatter.3
  86.4 24.9 all-gather.2
  116.6 47.6 all-gather.4
  174.9 167.2 all-reduce.1
where the time goes:
time: 412 us; the launch traced here: 411 us
  waiting for transfers between devices  278 us (67%)
  blocking collectives  58.3 us (14%)
  matrix products  43.8 us (11%)
  between operations  16.3 us (4%)
  other arithmetic  10.1 us (2%)
    psum x1, waiting for transfers between devices, local(): recon_all, gate_total = lax.psum((recon_part, gate_part), ('dp', 'mp'))  167 us
    all_gather x1, waiting for transfers between devices, local(): h_cols = lax.all_gather(column_rows, 'dp', axis=1, tiled=True)  47.5 us
    psum x1, blocking collectives, local(): recon_all, gate_total = lax.psum((recon_part, gate_part), ('dp', 'mp'))  40.4 us
    reduce_scatter x1, waiting for transfers between devices, local(): lax.psum_scatter(lax.dot_general(w_down, hidden, (((0,), (1,)), ((), ()))...  36.9 us
    all_gather x1, waiting for transfers between devices, local(): whole_out = lax.all_gather(out_share, 'mp', axis=0, tiled=True)  26.5 us
    all_gather x1, blocking collectives, local(): full_rows = lax.all_gather(residual_in, 'mp', axis=1, tiled=True)  17.8 us
    dot_general x1, matrix products, local(): lax.dot_general(w_down, hidden, (((0,), (1,)), ((), ())), preferred_eleme...  12.8 us
  transfers between devices with their start and end apart: 4, of which 4 were waited for; matrix products, arithmetic and copies ran while one was open for 0% of the time, Pallas kernels for 0%

commit v1 on v0

--- a/solution.py
+++ b/solution.py
@@ -47,7 +47,7 @@
     recon_part = lax.dot_general(
         w_dec, feat_bf, (((0,), (1,)), ((), ())), preferred_element_type=jnp.float32
     )
-    recon_all, gate_total = lax.psum((recon_part, gate_part), ("dp", "mp"))
+    recon_all, gate_total = lax.psum(lax.psum((recon_part, gate_part), "mp"), "dp")
     error_t = recon_all + b_dec[:, None] - h_cols.astype(jnp.float32)
     grad_bdec = jnp.sum(error_t, axis=1)
     square_total = jnp.sum(error_t * error_t)

time: 412 us -> 547 us (1.33)
  waiting for transfers between devices: 278 us -> 426 us
  blocking collectives: 58.3 us -> 44.2 us
    psum x1 -> x2, waiting for transfers between devices: 167 us -> 314 us  [the longest x1 159 us: local(): lax.psum(lax.psum((recon_part, gate_part), 'mp'), 'dp')]
    psum x1 -> x2, blocking collectives: 40.4 us -> 26.3 us  [the longest x1 16.8 us: local(): lax.psum((recon_part, gate_part), 'mp')]
  transfers between devices with their start and end apart: 4 -> 5, of which waited for: 4 -> 5; matrix products, arithmetic and copies ran while one was open for 0% -> 0% of each run, Pallas kernels for 0% -> 0%
where the time goes in v1:
time: 547 us; the launch traced here: 546 us
  waiting for transfers between devices  426 us (78%)
  matrix products  45.8 us (8%)
  blocking collectives  44.2 us (8%)
  between operations  16.3 us (3%)
  other arithmetic  10.1 us (2%)
    psum x1, waiting for transfers between devices, local(): lax.psum(lax.psum((recon_part, gate_part), 'mp'), 'dp')  159 us
    psum x1, waiting for transfers between devices, local(): lax.psum((recon_part, gate_part), 'mp')  156 us
    all_gather x1, waiting for transfers between devices, local(): h_cols = lax.all_gather(column_rows, 'dp', axis=1, tiled=True)  47.7 us
    reduce_scatter x1, waiting for transfers between devices, local(): lax.psum_scatter(lax.dot_general(w_down, hidden, (((0,), (1,)), ((), ()))...  37 us
    all_gather x1, waiting for transfers between devices, local(): whole_out = lax.all_gather(out_share, 'mp', axis=0, tiled=True)  26.5 us
    all_gather x1, blocking collectives, local(): full_rows = lax.all_gather(residual_in, 'mp', axis=1, tiled=True)  17.8 us
    psum x1, blocking collectives, local(): lax.psum((recon_part, gate_part), 'mp')  16.8 us
    dot_general x1, matrix products, local(): lax.dot_general(w_down, hidden, (((0,), (1,)), ((), ())), preferred_eleme...  12.7 us
  transfers between devices with their start and end apart: 5, of which 5 were waited for; matrix products, arithmetic and copies ran while one was open for 0% of the time, Pallas kernels for 0%

profile of v1, /device:TPU:0, one launch (start us, length us, event | category | flops | bytes accessed | tf_op | source)
XLA Modules:
  0.0 546.4 jit_solution(10705825602551404186)
XLA Ops:
  7.2 17.8 %all_gather.9 = bf16[128,3584]{0,1:T(8,128)(2,1)S(1)} all-gather(bf16[128,448]{0,1:T(8,128)(2,1)} %param.11), channel_id=1, replica_groups=mesh['dp'=4,'mp'=8] {'mp'}, dimensions={1}, use_global_device_ids=true | all-gather | bytes 1032192 | tf_op jit(solution)/shard_map/all_gather | solution.py:20
  25.1 0.5 copy.18
  25.6 0.3 fusion.5
  25.9 7.5 %fusion.25 = f32[128,1792]{1,0:T(8,128)} fusion(bf16[3584,1792]{1,0:T(8,128)(2,1)} %param.14, bf16[128,3584]{1,0:T(8,128)(2,1)S(1)} %copy.18, f32[3584]{0:T(1024)S(1)} %copy-done.1, f32[128]{0:T(128)S(1)} %add_rsqrt_fusion.1), kind=kOutput, calls=%fused_computation.40 | convolution fusion | flops 1646002176 | bytes 14694912 | tf_op jit(solution)/shard_map/dot_general | solution.py:27
  33.3 12.7 %convolution_bitcast_fusion.1 = f32[3584,128]{0,1:T(8,128)S(1)} fusion(bf16[1792,3584]{1,0:T(8,128)(2,1)} %param.16, bf16[3584,1792]{1,0:T(8,128)(2,1)} %param.15, f32[128,1792]{1,0:T(8,128)} %fusion.25, bf16[128,3584]{1,0:T(8,128)(2,1)S(1)} %copy.18, f32[3584]{0:T(1024)S(1)} %copy-done.1, f32[128]{0:T(128)S(1)} %add_rsqrt_fusion.1), kind=kOutput, calls=%fused_computation.5 | convolution fusion | flops 3292463104 | bytes 29374976 | tf_op jit(solution)/shard_map/dot_general | solution.py:31
  46.1 1.7 copy.21
  47.8 37.0 %reduce-scatter.4.cloned.1.call-done = f32[448,128]{1,0:T(8,128)} async-done(((f32[3584,128]{1,0:T(8,128)}), f32[448,128]{1,0:T(8,128)}) %reduce-scatter.4.cloned.1.call-update) | async-done | bytes 229392 | tf_op jit(solution)/shard_map/reduce_scatter | solution.py:30
  84.9 26.5 %all-gather.3.cloned.1.call-done = f32[3584,128]{1,0:T(8,128)} async-done(((f32[448,128]{1,0:T(8,128)}), f32[3584,128]{1,0:T(8,128)}) %all-gather.3.cloned.1.call-update) | async-done | bytes 1835024 | tf_op jit(solution)/shard_map/all_gather | solution.py:38
  111.4 2.0 multiply_reduce_fusion.1
  113.4 1.8 copy.20
  115.3 1.3 fusion.4
  116.6 47.7 %all-gather.5.cloned.1.call-done = bf16[3584,512]{0,1:T(8,128)(2,1)} async-done(((bf16[3584,128]{0,1:T(8,128)(2,1)}), bf16[3584,512]{0,1:T(8,128)(2,1)}) %all-gather.5.cloned.1.call-update) | async-done | bytes 3670032 | tf_op jit(solution)/shard_map/all_gather | solution.py:42
  164.3 5.3 convolution_add_fusion
  169.7 5.2 convolution_bitcast_fusion
  174.9 0.2 all-reduce.5.cloned.1.call-start
  175.1 155.7 %all-reduce.3.cloned.1.call-done = f32[3584,512]{0,1:T(8,128)} async-done(((f32[3584,512]{0,1:T(8,128)}), f32[3584,512]{0,1:T(8,128)}) %all-reduce.3.cloned.1.call-update) | async-done | bytes 7340048 | tf_op jit(solution)/shard_map/psum | solution.py:50
  330.8 158.7 %all-reduce.5.cloned.1.call-done = f32[3584,512]{0,1:T(8,128)} async-done(((f32[3584,512]{0,1:T(8,128)}), f32[3584,512]{0,1:T(8,128)}) %all-reduce.5.cloned.1.call-update) | async-done | bytes 7340048 | tf_op jit(solution)/shard_map/psum | solution.py:50
  489.5 5.9 %fusion.1 = (f32[3584]{0:T(1024)}, f32[]{:T(128)}, bf16[3584,512]{0,1:T(8,128)(2,1)S(1)}) fusion(bf16[3584,512]{0,1:T(8,128)(2,1)} %all-gather.5.cloned.1.call-done, f32[3584,512]{0,1:T(8,128)} %all-reduce.5.cloned.1.call-done, f32[3584]{0:T(1024)S(1)} %copy-done.3), kind=kLoop, calls=%fused_computation.11 | loop fusion | flops 12841471 | bytes 14708740 | tf_op jit(solution)/shard_map/reduce_sum | solution.py:52
  495.4 3.1 fusion.32
  498.5 16.8 %psum.30 = f32[]{:T(128)} all-reduce(f32[]{:T(128)} %get-tuple-element.13), channel_id=1, replica_groups=mesh['dp'=4,'mp'=8] {'mp'}, use_global_device_ids=true, to_apply=%region_7.0 | all-reduce | flops 1 | bytes 8 | tf_op jit(solution)/shard_map/psum | solution.py:50
  515.3 6.0 %convolution_convert_fusion = bf16[512,3584]{1,0:T(8,128)(2,1)} fusion(bf16[3584,512]{0,1:T(8,128)(2,1)} %copy-done, f32[512,512]{1,0:T(8,128)S(1)} %convolution_add_fusion, f32[512]{0:T(512)S(1)} %copy-done.7), kind=kOutput, calls=%fused_computation.3 | convolution fusion | flops 1882718208 | bytes 8390656 | tf_op jit(solution)/shard_map/dot_general | solution.py:58
  521.4 9.5 %psum.31 = f32[]{:T(128)} all-reduce(f32[]{:T(128)} %psum.30), channel_id=1, replica_groups=mesh['dp'=4,'mp'=8] {'dp'}, use_global_device_ids=true, to_apply=%region_8.0 | all-reduce | flops 1 | bytes 8 | tf_op jit(solution)/shard_map/psum | solution.py:50
  530.9 0.6 neg.7
  532.8 6.0 %convolution_convert_fusion.1 = bf16[3584,512]{1,0:T(8,128)(2,1)} fusion(bf16[3584,512]{0,1:T(8,128)(2,1)} %all-gather.5.cloned.1.call-done, bf16[512,512]{1,0:T(8,128)(2,1)S(1)} %get-tuple-element.11), kind=kOutput, calls=%fused_computation.4 | convolution fusion | flops 1880883200 | bytes 7864320 | tf_op jit(solution)/shard_map/dot_general | solution.py:69
  (27 shorter events, 0.3 us)
Async XLA Ops:
  7.2 18.7 %copy-start.1 = (f32[3584]{0:T(1024)S(1)}, f32[3584]{0:T(1024)}, u32[]{:S(2)}) copy-start(f32[3584]{0:T(1024)} %param.12) | copy-start | bytes 43012
  7.2 77.6 %reduce-scatter.4.cloned.1.call-start = ((), (), s32[]{:S(2)}) async-start(), calls=%async_computation.5 | async-start | bytes 2064384 | tf_op jit(solution)/shard_map/reduce_scatter | solution.py:30
  47.7 67.5 %copy-start.2 = (f32[3584]{0:T(1024)S(1)}, f32[3584]{0:T(1024)}, u32[]{:S(2)}) copy-start(f32[3584]{0:T(1024)} %param.13) | copy-start | bytes 43012
  47.8 63.7 %all-gather.3.cloned.1.call-start = ((), (), s32[]{:S(2)}) async-start(), calls=%async_computation.1 | async-start | bytes 2064384 | tf_op jit(solution)/shard_map/all_gather | solution.py:38
  84.8 79.5 %all-gather.5.cloned.1.call-start = ((), (), s32[]{:S(2)}) async-start(), calls=%async_computation.2 | async-start | bytes 4587520 | tf_op jit(solution)/shard_map/all_gather | solution.py:42
  113.4 50.9 %copy-start.6 = (f32[512]{0:T(512)S(1)}, f32[512]{0:T(512)}, u32[]{:S(2)}) copy-start(f32[512]{0:T(512)} %param.18) | copy-start | bytes 6148
  116.6 53.1 %copy-start.7 = (f32[512]{0:T(512)S(1)}, f32[512]{0:T(512)}, u32[]{:S(2)}) copy-start(f32[512]{0:T(512)} %param.19) | copy-start | bytes 6148
  116.6 214.2 %all-reduce.3.cloned.1.call-start = ((), (), s32[]{:S(2)}) async-start(), calls=%async_computation.3 | async-start | bytes 14680064 | tf_op jit(solution)/shard_map/psum | solution.py:50
  164.3 5.4 copy-start.4
  174.9 314.6 %all-reduce.5.cloned.1.call-start = ((), (), s32[]{:S(2)}) async-start(), calls=%async_computation.4 | async-start | bytes 14680064 | tf_op jit(solution)/shard_map/psum | solution.py:50
  330.8 158.7 %copy-start.3 = (f32[3584]{0:T(1024)S(1)}, f32[3584]{0:T(1024)}, u32[]{:S(2)}) copy-start(f32[3584]{0:T(1024)} %param.21) | copy-start | bytes 43012
  489.5 6.0 %copy-start.5 = (bf16[512,3584]{1,0:T(8,128)(2,1)S(1)}, bf16[512,3584]{1,0:T(8,128)(2,1)}, u32[]{:S(2)}) copy-start(bf16[512,3584]{1,0:T(8,128)(2,1)} %param.20) | copy-start | bytes 11010052
  495.4 3.1 copy-start
Sparse Core Ops, SparseCore 0:
  47.9 36.8 reduce-scatter.3
  86.5 24.9 all-gather.2
  116.7 47.6 all-gather.4
  175.0 155.7 all-reduce.2
  334.0 155.4 all-reduce.4
